TPU v7x, 32 devices: a whole 2x2x4 slice. The times are simulated.
32 devices in a mesh: cols: 8 (over z, y), grp: 4 (over x, core).
Axes of the slice: x: 2, y: 2, z: 4, core: 2. Of those that a mesh axis runs over, the one named last changes fastest.
Arguments:
- hcols: float32 [8, 4, 9, 128, 128], P('cols', 'grp'), as said below
- neighbours: int32 [8, 4, 6], P('cols', 'grp'), may hold values from 0 to 8, as said below
- counts: int32 [8, 4], P('cols', 'grp'), may hold values from 4 to 6, as said below
Outputs:
- density: float32 [8, 4, 9, 128, 128], P('cols', 'grp')
Inputs may be any that keep to these rules, and one draw needn't show every extreme that they name: `neighbours`: each list starts with 4 (the block column itself) and holds 6 distinct offset indices. Only the first counts entries of a list are used; some block column uses all 6. hcols describes a symmetric H as stated in the first step.
All inputs are finite; a program needn't handle non-finite values.
Results may differ from a plain program's by a relative error of at most 0.005.
Values sent between devices are 32-bit elements; how exact they have to be, the bound alone decides.
A program may use at most 64 MiB of HBM per device.

v0:
```python
import jax
import jax.numpy as jnp
from jax import lax
from jax.sharding import PartitionSpec as P

exact_mode = lax.Precision.HIGHEST


def padded(cells, sides, width):
    for axis, dim in sides:
        count = lax.axis_size(axis)
        head = lax.slice_in_dim(cells, 0, width, axis=dim)
        tail = lax.slice_in_dim(cells, cells.shape[dim] - width, cells.shape[dim], axis=dim)
        cells = jnp.concatenate(
            [
                lax.ppermute(tail, axis, [(i, (i + 1) % count) for i in range(count)]),
                cells,
                lax.ppermute(head, axis, [((i + 1) % count, i) for i in range(count)]),
            ],
            axis=dim,
        )
    return cells


def product(left, right):
    return jnp.dot(left, right, precision=exact_mode, preferred_element_type=jnp.float32)


def sign_column(matrix, spectral, block_width):
    initial = matrix / spectral
    square = product(initial, initial)
    iterate = 1.5 * initial - 0.5 * product(initial, square)
    column = iterate[:, :block_width]
    return 1.5 * column - 0.5 * product(iterate, product(iterate, column))


def assemble(beside_all, offset_ids, live_count, block_width):
    slot_count = offset_ids.shape[0]
    along_cols = offset_ids // 3 - 1
    along_grp = offset_ids % 3 - 1
    delta_cols = along_cols[:, None] - along_cols[None, :]
    delta_grp = along_grp[:, None] - along_grp[None, :]
    inside = (jnp.abs(delta_cols) <= 1) & (jnp.abs(delta_grp) <= 1)
    live_slots = jnp.arange(slot_count, dtype=jnp.int32) < live_count
    usable = inside & live_slots[:, None] & live_slots[None, :]
    stored = jnp.clip((delta_cols + 1) * 3 + (delta_grp + 1), 0, 8)
    flat_index = offset_ids[None, :] * 9 + stored
    stacked = beside_all.reshape(81, block_width, block_width)
    picked = jnp.take(stacked, flat_index.reshape(-1), axis=0)
    picked = picked.reshape(slot_count, slot_count, block_width, block_width)
    picked = jnp.where(usable[:, :, None, None], picked, jnp.float32(0.0))
    return picked.transpose(0, 2, 1, 3).reshape(slot_count * block_width, slot_count * block_width)


def scatter_out(dens_col, offset_ids, live_count, block_width):
    slot_count = offset_ids.shape[0]
    live_slots = jnp.arange(slot_count, dtype=jnp.int32) < live_count
    one_hot = (
        (offset_ids[:, None] == jnp.arange(9, dtype=jnp.int32)[None, :]) & live_slots[:, None]
    ).astype(jnp.float32)
    row_blocks = dens_col.reshape(slot_count, block_width, block_width)
    return jnp.einsum("pk,pab->kab", one_hot, row_blocks, precision=exact_mode)


def shards(hcols, neighbours, counts):
    block_width = hcols.shape[-1]
    sum_squares = lax.psum(jnp.sum(hcols * hcols), ("cols", "grp"))
    rows_total = block_width * lax.axis_size("cols") * lax.axis_size("grp")
    spectral = 2.0 * jnp.sqrt(sum_squares / rows_total + 1e-06)
    beside_all = padded(hcols, (("cols", 0), ("grp", 1)), 1)
    offset_ids = neighbours[0, 0]
    live_count = counts[0, 0]
    matrix = assemble(beside_all, offset_ids, live_count, block_width)
    sign_col = sign_column(matrix, spectral, block_width)
    identity_cols = jnp.eye(matrix.shape[0], block_width, dtype=jnp.float32)
    dens_col = 0.5 * (identity_cols - sign_col)
    return scatter_out(dens_col, offset_ids, live_count, block_width)[None, None]


def solution(mesh):
    in_specs = (P("cols", "grp", None, None, None), P("cols", "grp", None), P("cols", "grp"))
    out_specs = P("cols", "grp", None, None, None)
    return jax.shard_map(shards, mesh=mesh, in_specs=in_specs, out_specs=out_specs, check_vma=False)
```

profile of v0, /device:TPU:1, one launch (start us, length us, event | category | flops | bytes accessed | tf_op | source)
XLA Modules:
  0.0 134.1 jit_solution(11146282183493209535)
XLA Ops:
  0.0 2.1 %collective-permute-start = (f32[1,1,9,128,128]{4,3,2,1,0:T(8,128)}, f32[1,1,9,128,128]{4,3,2,1,0:T(8,128)S(1)}, u32[]{:S(2)}, u32[]{:S(2)}) collective-permute-start(f32[1,1,9,128,128]{4,3,2,1,0:T(8,128)} %param.3), channel_id=1, source_target_pairs={{0,4},{4,8},{8,12},{12,16},{16,20},{20,24},{24,28},{28,0},{1,5},{5... | collective-permute-start | bytes 1769480 | tf_op jit(solution)/shard_map/ppermute | solution.py:16
  2.1 3.1 %collective-permute-start.1 = (f32[1,1,9,128,128]{4,3,2,1,0:T(8,128)}, f32[1,1,9,128,128]{4,3,2,1,0:T(8,128)S(1)}, u32[]{:S(2)}, u32[]{:S(2)}) collective-permute-start(f32[1,1,9,128,128]{4,3,2,1,0:T(8,128)} %param.3), channel_id=1, source_target_pairs={{4,0},{8,4},{12,8},{16,12},{20,16},{24,20},{28,24},{0,28},{5,1},{9... | collective-permute-start | bytes 1769480 | tf_op jit(solution)/shard_map/ppermute | solution.py:18
  5.2 21.9 %collective-permute-done = f32[1,1,9,128,128]{4,3,2,1,0:T(8,128)S(1)} collective-permute-done((f32[1,1,9,128,128]{4,3,2,1,0:T(8,128)}, f32[1,1,9,128,128]{4,3,2,1,0:T(8,128)S(1)}, u32[]{:S(2)}, u32[]{:S(2)}) %collective-permute-start) | collective-permute-done | bytes 589856 | tf_op jit(solution)/shard_map/ppermute | solution.py:16
  27.1 1.9 %multiply_reduce_fusion = (f32[]{:T(128)}, f32[3,1,9,128,128]{4,3,2,1,0:T(8,128)S(1)}) fusion(f32[1,1,9,128,128]{4,3,2,1,0:T(8,128)} %param.3, f32[3,1,9,128,128]{4,3,2,1,0:T(8,128)S(1)} %constant_dynamic-update-slice_fusion.2), kind=kLoop, calls=%fused_computation.16 | loop fusion | flops 294911 | bytes 1179652 | tf_op jit(solution)/shard_map/reduce_sum | solution.py:67
  29.0 0.0 collective-permute-done.1
  29.0 2.8 %collective-permute-start.2 = (f32[3,1,9,128,128]{4,3,2,1,0:T(8,128)S(1)}, f32[3,1,9,128,128]{4,3,2,1,0:T(8,128)S(1)}, u32[]{:S(2)}, u32[]{:S(2)}) collective-permute-start(f32[3,1,9,128,128]{4,3,2,1,0:T(8,128)S(1)} %constant_dynamic-update-slice_fusion), channel_id=1, source_target_pairs={{0,1},{1,2},{2,3},{3,0},{4,5},{5,6},{6,7},{7,4},{8,9},{9,10},{10,1... | collective-permute-start | bytes 5308424 | tf_op jit(solution)/shard_map/ppermute | solution.py:16
  31.9 0.0 collective-permute-start.3
  31.9 0.5 copy-done
  32.4 0.1 fusion.19
  32.5 0.6 reshape.273
  33.7 0.7 fusion.30
  34.4 1.3 fusion.23
  35.6 69.8 %psum.7 = f32[]{:T(128)} all-reduce(f32[]{:T(128)} %get-tuple-element.5), channel_id=1, replica_groups=mesh['cols'=8,'grp'=4] {'cols','grp'}, use_global_device_ids=true, to_apply=%region_1.0 | all-reduce | flops 1 | bytes 8 | tf_op jit(solution)/shard_map/psum | solution.py:67
  106.1 4.2 %pad_maximum_fusion = f32[3,3,9,128,128]{4,3,2,1,0:T(8,128)} fusion(f32[3,1,9,128,128]{4,3,2,1,0:T(8,128)} %collective-permute-done.3, f32[3,1,9,128,128]{4,3,2,1,0:T(8,128)S(1)} %constant_dynamic-update-slice_fusion, f32[3,1,9,128,128]{4,3,2,1,0:T(8,128)S(1)} %collective-permute-done.2), kind=kLoop, calls=%fused_computation.1 | loop fusion | flops 2654208 | bytes 10616832 | tf_op jit(solution)/shard_map/concatenate | solution.py:14
  110.3 3.2 %gather_fusion = f32[36,128,128]{2,1,0:T(8,128)S(1)} fusion(f32[81,128,128]{2,1,0:T(8,128)} %bitcast.34, s32[1024]{0:T(1024)S(1)} %pad_clamp_fusion), kind=kCustom, calls=%fused_computation | custom fusion | bytes 4718736 | tf_op jit(solution)/shard_map/jit(_take)/gather | solution.py:49
  113.6 0.5 divide_bitcast_fusion
  114.1 1.4 %copy.6 = f32[6,128,6,128]{3,2,1,0:T(8,128)S(1)} copy(f32[6,128,6,128]{3,1,2,0:T(8,128)S(1)} %divide_bitcast_fusion) | data formatting | bytes 4718592 | tf_op jit(solution)/shard_map/div | solution.py:30
  115.5 6.3 %fusion.2 = f32[768,768]{1,0:T(8,128)S(1)} fusion(f32[96,8,6,128]{3,2,1,0:T(8,128)S(1)} %bitcast.35), kind=kOutput, calls=%fused_computation.4 | convolution fusion | flops 5435817984 | bytes 4718592 | tf_op jit(solution)/shard_map/dot_general | solution.py:26
  121.7 6.5 %fusion.4 = f32[768,768]{1,0:T(8,128)S(1)} fusion(f32[768,768]{1,0:T(8,128)S(1)} %fusion.2, f32[96,8,6,128]{3,2,1,0:T(8,128)S(1)} %bitcast.36), kind=kOutput, calls=%fused_computation.7 | convolution fusion | flops 5437587456 | bytes 7077888 | tf_op jit(solution)/shard_map/dot_general | solution.py:26
  128.2 2.0 %fusion.13 = f32[768,128]{1,0:T(8,128)S(1)} fusion(f32[768,768]{1,0:T(8,128)S(1)} %fusion.4), kind=kOutput, calls=%fused_computation.19 | convolution fusion | flops 905969664 | bytes 3145728 | tf_op jit(solution)/shard_map/dot_general | solution.py:26
  130.2 0.0 copy-start.4
  130.2 2.0 %fusion.11 = f32[768,128]{1,0:T(8,128)S(1)} fusion(f32[768,768]{1,0:T(8,128)S(1)} %fusion.4, f32[768,128]{1,0:T(8,128)S(1)} %fusion.13), kind=kOutput, calls=%fused_computation.15 | convolution fusion | flops 906657792 | bytes 3538944 | tf_op jit(solution)/shard_map/dot_general | solution.py:26
  132.3 0.9 convolution_bitcast_fusion
  133.1 1.0 copy.8
  (15 shorter events, 0.1 us)
Async XLA Ops:
  0.0 31.9 %copy-start.3 = (s32[1,1,6]{2,1,0:T(1,128)S(1)}, s32[1,1,6]{2,1,0:T(1,128)}, u32[]{:S(2)}) copy-start(s32[1,1,6]{2,1,0:T(1,128)} %param.4) | copy-start | bytes 76
  0.0 27.0 %collective-permute-start = (f32[1,1,9,128,128]{4,3,2,1,0:T(8,128)}, f32[1,1,9,128,128]{4,3,2,1,0:T(8,128)S(1)}, u32[]{:S(2)}, u32[]{:S(2)}) collective-permute-start(f32[1,1,9,128,128]{4,3,2,1,0:T(8,128)} %param.3), channel_id=1, source_target_pairs={{0,4},{4,8},{8,12},{12,16},{16,20},{20,24},{24,28},{28,0},{1,5},{5... | collective-permute-start | bytes 1769480 | tf_op jit(solution)/shard_map/ppermute | solution.py:16
  2.1 26.9 %collective-permute-start.1 = (f32[1,1,9,128,128]{4,3,2,1,0:T(8,128)}, f32[1,1,9,128,128]{4,3,2,1,0:T(8,128)S(1)}, u32[]{:S(2)}, u32[]{:S(2)}) collective-permute-start(f32[1,1,9,128,128]{4,3,2,1,0:T(8,128)} %param.3), channel_id=1, source_target_pairs={{4,0},{8,4},{12,8},{16,12},{20,16},{24,20},{28,24},{0,28},{5,1},{9... | collective-permute-start | bytes 1769480 | tf_op jit(solution)/shard_map/ppermute | solution.py:18
  29.0 77.1 %collective-permute-start.2 = (f32[3,1,9,128,128]{4,3,2,1,0:T(8,128)S(1)}, f32[3,1,9,128,128]{4,3,2,1,0:T(8,128)S(1)}, u32[]{:S(2)}, u32[]{:S(2)}) collective-permute-start(f32[3,1,9,128,128]{4,3,2,1,0:T(8,128)S(1)} %constant_dynamic-update-slice_fusion), channel_id=1, source_target_pairs={{0,1},{1,2},{2,3},{3,0},{4,5},{5,6},{6,7},{7,4},{8,9},{9,10},{10,1... | collective-permute-start | bytes 5308424 | tf_op jit(solution)/shard_map/ppermute | solution.py:16
  31.9 74.2 %collective-permute-start.3 = (f32[3,1,9,128,128]{4,3,2,1,0:T(8,128)S(1)}, f32[3,1,9,128,128]{4,3,2,1,0:T(8,128)}, u32[]{:S(2)}, u32[]{:S(2)}) collective-permute-start(f32[3,1,9,128,128]{4,3,2,1,0:T(8,128)S(1)} %constant_dynamic-update-slice_fusion), channel_id=1, source_target_pairs={{1,0},{2,1},{3,2},{0,3},{5,4},{6,5},{7,6},{4,7},{9,8},{10,9},{11,1... | collective-permute-start | bytes 5308424 | tf_op jit(solution)/shard_map/ppermute | solution.py:18
  31.9 0.5 copy-start
  110.3 3.2 %copy-start.1 = (pred[6,6]{1,0:T(8,128)(4,1)S(1)}, pred[6,6]{1,0:T(8,128)(4,1)}, u32[]{:S(2)}) copy-start(pred[6,6]{1,0:T(8,128)(4,1)} %get-tuple-element.7) | copy-start | bytes 112
  110.3 3.2 %copy-start.2 = (pred[6,6]{1,0:T(8,128)(4,1)S(1)}, pred[6,6]{1,0:T(8,128)(4,1)}, u32[]{:S(2)}) copy-start(pred[6,6]{1,0:T(8,128)(4,1)} %get-tuple-element.8) | copy-start | bytes 112
  130.2 2.0 %copy-start.4 = (s32[1,1,6]{2,1,0:T(1,128)S(1)}, s32[1,1,6]{2,1,0:T(1,128)}, u32[]{:S(2)}) copy-start(s32[1,1,6]{2,1,0:T(1,128)} %param.4) | copy-start | bytes 76
where the time goes:
time: 136 us; the launch traced here: 134 us
  blocking collectives  69.8 us (51%)
  waiting for transfers between devices  21.9 us (16%)
  matrix products  17.6 us (13%)
  other arithmetic  8.63 us (6%)
  starting transfers between devices  7.99 us (6%)
  local copies, waits for them, and re-layouts  6.79 us (5%)
  between operations  1.41 us (1%)
    psum x1, blocking collectives, shards(): sum_squares = lax.psum(jnp.sum(hcols * hcols), ('cols', 'grp'))  69.8 us
    ppermute x2, waiting for transfers between devices, padded(): lax.ppermute(tail, axis, [(i, (i + 1) % count) for i in range(count)])  21.9 us
    dot_general x4, matrix products, product(): jnp.dot(left, right, precision=exact_mode, preferred_element_type=jnp.flo...  16.8 us
    ppermute x2, starting transfers between devices, padded(): lax.ppermute(tail, axis, [(i, (i + 1) % count) for i in range(count)])  4.9 us
    concatenate x1, other arithmetic, padded(): jnp.concatenate([lax.ppermute(tail, axis, [(i, (i + 1) % count) for i in...  4.23 us
    gather x1, local copies, waits for them, and re-layouts, assemble(): picked = jnp.take(stacked, flat_index.reshape(-1), axis=0)  3.22 us
    ppermute x2, starting transfers between devices, padded(): lax.ppermute(head, axis, [((i + 1) % count, i) for i in range(count)])  3.09 us
  transfers between devices with their start and end apart: 4, of which 1 were waited for; matrix products, arithmetic and copies ran while one was open for 3% of the time, Pallas kernels for 0%

commit v1 on v0

v1 whole, which is shorter than its diff:
```python
import functools

import jax
import jax.numpy as jnp
from jax import lax
from jax.experimental import pallas as pl
from jax.experimental.pallas import tpu as pltpu
from jax.sharding import PartitionSpec as P

MESH = pl.DeviceIdType.MESH
SLOTS = 6
STENCIL = 9
MISSING = 64
TURNED = 32


def transfers():
    plan = []
    for along_cols in (-1, 1):
        plan.append(((along_cols, 0), 3, 3))
    for along_cols in (-1, 1):
        for along_grp in (-1, 1):
            plan.append(((along_cols, along_grp), 4, 1))
    for along_grp, runs in ((1, ((0, 2), (4, 1), (6, 2))), (-1, ((1, 2), (4, 1), (7, 2)))):
        for first, blocks in runs:
            plan.append(((0, along_grp), first, blocks))
    placed, slot = [], STENCIL
    for offset, first, blocks in plan:
        placed.append((offset, first, blocks, slot))
        slot += blocks
    return placed, slot


def lookup(placed):
    table = [MISSING] * (STENCIL * STENCIL)
    held = [((0, 0), k, k) for k in range(STENCIL)]
    for offset, first, blocks, slot in placed:
        held += [(offset, first + i, slot + i) for i in range(blocks)]
    for (cols, grp), k, slot in held:
        row_cols, row_grp = cols + k // 3 - 1, grp + k % 3 - 1
        assert abs(row_cols) <= 1 and abs(row_grp) <= 1
        column = (cols + 1) * 3 + grp + 1
        row = (row_cols + 1) * 3 + row_grp + 1
        table[row * STENCIL + column] = slot
        if row != column:
            table[column * STENCIL + row] = slot + TURNED
    return table


def kernel(
    n_cols, n_grp, hcols, nbr, cnt, out, blk, table, high, low, dens, row_sums, col_sums,
    load_sem, send_sem, recv_sem, row_send, row_recv, col_send, col_recv,
):
    width = blk.shape[-1]
    placed, _ = transfers()
    col, grp = lax.axis_index("cols"), lax.axis_index("grp")

    def at(step_cols, step_grp):
        return (lax.rem(col + step_cols + n_cols, n_cols), lax.rem(grp + step_grp + n_grp, n_grp))

    load = pltpu.make_async_copy(hcols.at[0, 0], blk.at[pl.ds(0, STENCIL)], load_sem)
    load.start()
    barrier = pltpu.get_barrier_semaphore()

    def greet_row(i, carry):
        pl.semaphore_signal(barrier, inc=1, device_id=at(0, i), device_id_type=MESH)
        return carry

    def greet_col(i, carry):
        pl.semaphore_signal(barrier, inc=1, device_id=at(i, 0), device_id_type=MESH)
        return carry

    lax.fori_loop(1, n_grp, greet_row, 0)
    lax.fori_loop(1, n_cols, greet_col, 0)
    for step_cols in (-1, 1):
        for step_grp in (-1, 1):
            pl.semaphore_signal(
                barrier, inc=1, device_id=at(step_cols, step_grp), device_id_type=MESH
            )
    for i, value in enumerate(lookup(placed)):
        table[i] = jnp.int32(value)
    load.wait()
    own = jnp.zeros((8, width), jnp.float32)
    for k in range(STENCIL):
        part = blk[k]
        own = own + jnp.sum((part * part).reshape(width // 8, 8, width), axis=0)
    row_sums[0] = own
    pl.semaphore_wait(barrier, n_grp + n_cols + 2)

    def row_copy(i):
        return pltpu.make_async_remote_copy(
            src_ref=row_sums.at[0], dst_ref=row_sums.at[i], send_sem=row_send.at[i],
            recv_sem=row_recv.at[i], device_id=at(0, i), device_id_type=MESH,
        )

    def col_copy(i):
        return pltpu.make_async_remote_copy(
            src_ref=col_sums.at[0], dst_ref=col_sums.at[i], send_sem=col_send.at[i],
            recv_sem=col_recv.at[i], device_id=at(i, 0), device_id_type=MESH,
        )

    def start_row(i, carry):
        row_copy(i).start()
        return carry

    def start_col(i, carry):
        col_copy(i).start()
        return carry

    def wait_row(i, carry):
        row_copy(i).wait_recv()
        return carry

    def wait_col(i, carry):
        col_copy(i).wait_recv()
        return carry

    lax.fori_loop(1, n_grp, start_row, 0)
    copies = []
    for i, ((step_cols, step_grp), first, blocks, slot) in enumerate(placed):
        copy = pltpu.make_async_remote_copy(
            src_ref=blk.at[pl.ds(first, blocks)], dst_ref=blk.at[pl.ds(slot, blocks)],
            send_sem=send_sem.at[i], recv_sem=recv_sem.at[i],
            device_id=at(-step_cols, -step_grp), device_id_type=MESH,
        )
        copy.start()
        copies.append(copy)

    lax.fori_loop(1, n_grp, wait_row, 0)
    col_sums[0] = jnp.sum(row_sums[...], axis=0)
    lax.fori_loop(1, n_cols, start_col, 0)
    lax.fori_loop(1, n_cols, wait_col, 0)
    sum_squares = jnp.sum(jnp.sum(col_sums[...], axis=0), keepdims=True)
    rows_total = width * n_cols * n_grp
    inverse = 0.5 * lax.rsqrt(sum_squares / rows_total + 1e-06)

    count = cnt[0, 0]
    ids = [nbr[0, 0, p] for p in range(SLOTS)]

    def put(p, q, value):
        top = value.astype(jnp.bfloat16)
        rows, columns = pl.ds(p * width, width), pl.ds(q * width, width)
        high[rows, columns] = top
        low[rows, columns] = (value - top.astype(jnp.float32)).astype(jnp.bfloat16)

    for copy in copies:
        copy.wait_recv()

    for p in range(SLOTS):
        for q in range(p + 1):
            code = table[ids[p] * STENCIL + ids[q]]
            usable = (code < MISSING) & (p < count)
            turned = (code >= TURNED) & (code < MISSING)
            slot = lax.rem(code, TURNED)
            block = blk[slot]
            block = jnp.where(usable, block, 0.0)
            if p == q:
                put(p, q, block)
            else:
                other = block.T
                put(p, q, jnp.where(turned, other, block))
                put(q, p, jnp.where(turned, block, other))

    def times(vector):
        top = vector.astype(jnp.bfloat16)
        rest = (vector - top.astype(jnp.float32)).astype(jnp.bfloat16)
        both = jnp.concatenate([top, rest], axis=1)
        main = jnp.dot(high[...], both, preferred_element_type=jnp.float32)
        side = jnp.dot(low[...], top, preferred_element_type=jnp.float32)
        return (main[:, :width] + (main[:, width:] + side)) * inverse

    first = high[:, pl.ds(0, width)].astype(jnp.float32) + low[:, pl.ds(0, width)].astype(jnp.float32)
    initial = first * inverse
    column = 1.5 * initial - 0.5 * times(times(initial))
    image = column
    for _ in range(2):
        once = times(image)
        image = 1.5 * once - 0.5 * times(times(once))
    sign = 1.5 * column - 0.5 * image
    diagonal = lax.broadcasted_iota(jnp.int32, sign.shape, 0) == lax.broadcasted_iota(
        jnp.int32, sign.shape, 1
    )
    dens[...] = (0.5 * (jnp.where(diagonal, 1.0, 0.0) - sign)).reshape(dens.shape)

    for k in range(STENCIL):
        place, named = jnp.int32(0), jnp.int32(0)
        for p in range(SLOTS):
            hit = ((ids[p] == k) & (p < count)).astype(jnp.int32)
            place, named = place + p * hit, named + hit
        out[0, 0, k] = jnp.where(named > 0, dens[place], 0.0)

    def done_row(i, carry):
        row_copy(i).wait_send()
        return carry

    def done_col(i, carry):
        col_copy(i).wait_send()
        return carry

    for copy in copies:
        copy.wait_send()
    lax.fori_loop(1, n_grp, done_row, 0)
    lax.fori_loop(1, n_cols, done_col, 0)


def shards(hcols, neighbours, counts, n_cols, n_grp):
    width = hcols.shape[-1]
    placed, slots = transfers()
    order = SLOTS * width
    dma = pltpu.SemaphoreType.DMA
    return pl.pallas_call(
        functools.partial(kernel, n_cols, n_grp),
        out_shape=jax.ShapeDtypeStruct(hcols.shape, jnp.float32),
        in_specs=[
            pl.BlockSpec(memory_space=pl.ANY),
            pl.BlockSpec(memory_space=pltpu.SMEM),
            pl.BlockSpec(memory_space=pltpu.SMEM),
        ],
        out_specs=pl.BlockSpec(memory_space=pltpu.VMEM),
        scratch_shapes=[
            pltpu.VMEM((slots, width, width), jnp.float32),
            pltpu.SMEM((STENCIL * STENCIL,), jnp.int32),
            pltpu.VMEM((order, order), jnp.bfloat16),
            pltpu.VMEM((order, order), jnp.bfloat16),
            pltpu.VMEM((SLOTS, width, width), jnp.float32),
            pltpu.VMEM((n_grp, 8, width), jnp.float32),
            pltpu.VMEM((n_cols, 8, width), jnp.float32),
            dma,
            dma((len(placed),)),
            dma((len(placed),)),
            dma((n_grp,)),
            dma((n_grp,)),
            dma((n_cols,)),
            dma((n_cols,)),
        ],
        compiler_params=pltpu.CompilerParams(
            collective_id=0, has_side_effects=True, vmem_limit_bytes=32 * 1024 * 1024
        ),
        name="density_columns",
    )(hcols, neighbours, counts)


def solution(mesh):
    in_specs = (P("cols", "grp", None, None, None), P("cols", "grp", None), P("cols", "grp"))
    out_specs = P("cols", "grp", None, None, None)
    body = functools.partial(shards, n_cols=mesh.shape["cols"], n_grp=mesh.shape["grp"])
    return jax.shard_map(body, mesh=mesh, in_specs=in_specs, out_specs=out_specs, check_vma=False)
```

time: 136 us -> 30.8 us (0.23)
  the two profiles are of different devices: /device:TPU:1 before, /device:TPU:0 now
where the time goes in v1:
time: 30.8 us; the launch traced here: 30.7 us
  Pallas kernels  28.1 us (91%)
  local copies, waits for them, and re-layouts  1.88 us (6%)
  between operations  0.69 us (2%)
    pallas_call x1, Pallas kernels, shards(): pl.pallas_call(functools.partial(kernel, n_cols, n_grp), out_shape=jax.Sh...  28.1 us
    unnamed x5, local copies, waits for them, and re-layouts  1.88 us

profile of v1, /device:TPU:0, one launch (start us, length us, event | category | flops | bytes accessed | tf_op | source)
XLA Modules:
  0.0 30.7 jit_solution(3290440070592991084)
XLA Ops:
  0.0 0.0 copy-start.1
  0.7 0.0 copy-done.1
  0.7 0.0 copy-start
  0.7 1.1 %copy-done = f32[1,1,9,128,128]{4,3,2,1,0:T(8,128)S(1)} copy-done((f32[1,1,9,128,128]{4,3,2,1,0:T(8,128)S(1)}, f32[1,1,9,128,128]{4,3,2,1,0:T(8,128)}, u32[]{:S(2)}) %copy-start) | copy-done | bytes 589848
  1.7 28.1 %density_columns.1 = f32[1,1,9,128,128]{4,3,2,1,0:T(8,128)S(1)} custom-call(f32[1,1,9,128,128]{4,3,2,1,0:T(8,128)S(1)} %copy-done, s32[1,1,6]{2,1,0:T(1,128)S(1)} %copy-done.1, s32[1,1]{1,0:T(1,128)S(6)} %copy.5.cnt), custom_call_target="tpu_custom_call" | custom-call | tf_op jit(solution)/shard_map/density_columns/pallas_call | solution.py:211
  29.9 0.8 %copy.6 = f32[1,1,9,128,128]{4,3,2,1,0:T(8,128)} copy(f32[1,1,9,128,128]{4,3,2,1,0:T(8,128)S(1)} %density_columns.1) | data formatting | bytes 1179648
Async XLA Ops:
  0.0 0.7 %copy-start.1 = (s32[1,1,6]{2,1,0:T(1,128)S(1)}, s32[1,1,6]{2,1,0:T(1,128)}, u32[]{:S(2)}) copy-start(s32[1,1,6]{2,1,0:T(1,128)} %nbr.1) | copy-start | bytes 76
  0.7 1.1 %copy-start = (f32[1,1,9,128,128]{4,3,2,1,0:T(8,128)S(1)}, f32[1,1,9,128,128]{4,3,2,1,0:T(8,128)}, u32[]{:S(2)}) copy-start(f32[1,1,9,128,128]{4,3,2,1,0:T(8,128)} %hcols.1) | copy-start | bytes 1769476

commit v2 on v1

--- a/solution.py
+++ b/solution.py
@@ -48,8 +48,8 @@
 
 
 def kernel(
-    n_cols, n_grp, hcols, nbr, cnt, out, blk, table, high, low, dens, row_sums, col_sums,
-    load_sem, send_sem, recv_sem, row_send, row_recv, col_send, col_recv,
+    n_cols, n_grp, hcols, nbr_hbm, cnt_hbm, out, nbr, cnt, blk, table, high, low, dens, row_sums, col_sums,
+    small_sem, load_sem, send_sem, recv_sem, row_send, row_recv, col_send, col_recv,
 ):
     width = blk.shape[-1]
     placed, _ = transfers()
@@ -58,8 +58,18 @@
     def at(step_cols, step_grp):
         return (lax.rem(col + step_cols + n_cols, n_cols), lax.rem(grp + step_grp + n_grp, n_grp))
 
+    odd = lax.rem(grp, 2)
+    side = 1 - 2 * odd
+    straight = {offset[0]: slot for offset, _, _, slot in placed if offset[1] == 0}
+    corner = {offset: slot for offset, _, _, slot in placed if 0 not in offset}
     load = pltpu.make_async_copy(hcols.at[0, 0], blk.at[pl.ds(0, STENCIL)], load_sem)
     load.start()
+    small = [
+        pltpu.make_async_copy(nbr_hbm, nbr, small_sem.at[0]),
+        pltpu.make_async_copy(cnt_hbm, cnt, small_sem.at[1]),
+    ]
+    for copy in small:
+        copy.start()
     barrier = pltpu.get_barrier_semaphore()
 
     def greet_row(i, carry):
@@ -79,6 +89,14 @@
             )
     for i, value in enumerate(lookup(placed)):
         table[i] = jnp.int32(value)
+    even = 1 - odd
+    for swapped, step_cols, step_grp in ((even, -1, 1), (odd, 1, -1)):
+        near, far = (step_cols + 1) * 3 + 1, (step_cols + 1) * 3 + step_grp + 1
+        place = straight[step_cols] + step_grp + 1
+        table[far * STENCIL + near] = place + TURNED * swapped
+        table[near * STENCIL + far] = place + TURNED * (1 - swapped)
+    for copy in small:
+        copy.wait()
     load.wait()
     own = jnp.zeros((8, width), jnp.float32)
     for k in range(STENCIL):
@@ -117,22 +135,32 @@
 
     lax.fori_loop(1, n_grp, start_row, 0)
     copies = []
-    for i, ((step_cols, step_grp), first, blocks, slot) in enumerate(placed):
+
+    def push(source, target, blocks, step_cols, step_grp):
+        i = len(copies)
         copy = pltpu.make_async_remote_copy(
-            src_ref=blk.at[pl.ds(first, blocks)], dst_ref=blk.at[pl.ds(slot, blocks)],
+            src_ref=blk.at[pl.ds(source, blocks)], dst_ref=blk.at[pl.ds(target, blocks)],
             send_sem=send_sem.at[i], recv_sem=recv_sem.at[i],
-            device_id=at(-step_cols, -step_grp), device_id_type=MESH,
+            device_id=at(step_cols, step_grp), device_id_type=MESH,
         )
         copy.start()
         copies.append(copy)
+        return copy
+
+    def pick(at_even, at_odd):
+        return at_even + (at_odd - at_even) * odd
+
+    whole_edge = push(3, pick(straight[1], straight[-1]), 3, -side, 0)
+    half_edge = push(3 + odd, pick(straight[-1], straight[1]) + odd, 2, side, 0)
+    for step_cols in (-1, 1):
+        push(4, pick(corner[-step_cols, 1], corner[-step_cols, -1]), 1, step_cols, -side)
+    for offset, first, blocks, slot in placed:
+        if offset[0] == 0:
+            push(first, slot, blocks, 0, -offset[1])
 
     lax.fori_loop(1, n_grp, wait_row, 0)
     col_sums[0] = jnp.sum(row_sums[...], axis=0)
     lax.fori_loop(1, n_cols, start_col, 0)
-    lax.fori_loop(1, n_cols, wait_col, 0)
-    sum_squares = jnp.sum(jnp.sum(col_sums[...], axis=0), keepdims=True)
-    rows_total = width * n_cols * n_grp
-    inverse = 0.5 * lax.rsqrt(sum_squares / rows_total + 1e-06)
 
     count = cnt[0, 0]
     ids = [nbr[0, 0, p] for p in range(SLOTS)]
@@ -143,8 +171,20 @@
         high[rows, columns] = top
         low[rows, columns] = (value - top.astype(jnp.float32)).astype(jnp.bfloat16)
 
+    whole_edge.wait_recv()
+    push(
+        pick(straight[1] + 1, straight[-1] + 1), pick(corner[1, -1], corner[-1, 1]), 1, 0, side
+    )
+    push(
+        pick(straight[1] + 2, straight[-1]), pick(straight[1], straight[-1] + 2), 1, 0, side
+    )
+    half_edge.wait_recv()
+    push(
+        pick(straight[-1] + 1, straight[1] + 1), pick(corner[-1, -1], corner[1, 1]), 1, 0, side
+    )
     for copy in copies:
-        copy.wait_recv()
+        if copy is not whole_edge and copy is not half_edge:
+            copy.wait_recv()
 
     for p in range(SLOTS):
         for q in range(p + 1):
@@ -161,6 +201,11 @@
                 put(p, q, jnp.where(turned, other, block))
                 put(q, p, jnp.where(turned, block, other))
 
+    lax.fori_loop(1, n_cols, wait_col, 0)
+    sum_squares = jnp.sum(jnp.sum(col_sums[...], axis=0), keepdims=True)
+    rows_total = width * n_cols * n_grp
+    inverse = 0.5 * lax.rsqrt(sum_squares / rows_total + 1e-06)
+
     def times(vector):
         top = vector.astype(jnp.bfloat16)
         rest = (vector - top.astype(jnp.float32)).astype(jnp.bfloat16)
@@ -212,12 +257,14 @@
         functools.partial(kernel, n_cols, n_grp),
         out_shape=jax.ShapeDtypeStruct(hcols.shape, jnp.float32),
         in_specs=[
-            pl.BlockSpec(memory_space=pl.ANY),
-            pl.BlockSpec(memory_space=pltpu.SMEM),
-            pl.BlockSpec(memory_space=pltpu.SMEM),
+            pl.BlockSpec(memory_space=pltpu.HBM),
+            pl.BlockSpec(memory_space=pltpu.HBM),
+            pl.BlockSpec(memory_space=pltpu.HBM),
         ],
         out_specs=pl.BlockSpec(memory_space=pltpu.VMEM),
         scratch_shapes=[
+            pltpu.SMEM(neighbours.shape, jnp.int32),
+            pltpu.SMEM(counts.shape, jnp.int32),
             pltpu.VMEM((slots, width, width), jnp.float32),
             pltpu.SMEM((STENCIL * STENCIL,), jnp.int32),
             pltpu.VMEM((order, order), jnp.bfloat16),
@@ -225,16 +272,17 @@
             pltpu.VMEM((SLOTS, width, width), jnp.float32),
             pltpu.VMEM((n_grp, 8, width), jnp.float32),
             pltpu.VMEM((n_cols, 8, width), jnp.float32),
+            dma((2,)),
             dma,
-            dma((len(placed),)),
-            dma((len(placed),)),
+            dma((len(placed) + 1,)),
+            dma((len(placed) + 1,)),
             dma((n_grp,)),
             dma((n_grp,)),
             dma((n_cols,)),
             dma((n_cols,)),
         ],
         compiler_params=pltpu.CompilerParams(
-            collective_id=0, has_side_effects=True, vmem_limit_bytes=32 * 1024 * 1024
+            collective_id=0, has_side_effects=True, vmem_limit_bytes=63 * 1024 * 1024
         ),
         name="density_columns",
     )(hcols, neighbours, counts)

time: 30.8 us -> 28.5 us (0.925)
  the two profiles are of different devices: /device:TPU:0 before, /device:TPU:1 now
where the time goes in v2:
time: 28.5 us; the launch traced here: 28.1 us
  Pallas kernels  25.5 us (89%)
  local copies, waits for them, and re-layouts  1.92 us (7%)
  between operations  0.66 us (2%)
    pallas_call x1, Pallas kernels, shards(): pl.pallas_call(functools.partial(kernel, n_cols, n_grp), out_shape=jax.Sh...  25.5 us
    unnamed x1, local copies, waits for them, and re-layouts  1.92 us

profile of v2, /device:TPU:1, one launch (start us, length us, event | category | flops | bytes accessed | tf_op | source)
XLA Modules:
  0.0 28.1 jit_solution(4444491023796700573)
XLA Ops:
  0.7 25.5 %density_columns.1 = f32[1,1,9,128,128]{4,3,2,1,0:T(8,128)} custom-call(f32[1,1,9,128,128]{4,3,2,1,0:T(8,128)} %hcols.1, s32[1,1,6]{2,1,0:T(1,128)} %nbr_hbm.1, s32[1,1]{1,0:T(1,128)S(6)} %copy.5.cnt_hbm), custom_call_target="tpu_custom_call" | custom-call | tf_op jit(solution)/shard_map/density_columns/pallas_call | solution.py:256
  26.1 1.9 %copy.6 = f32[1,1,9,128,128]{4,3,2,1,0:T(8,128)} copy(f32[1,1,9,128,128]{4,3,2,1,0:T(8,128)} %density_columns.1) | data formatting | bytes 1179648

commit v3 on v2

--- a/solution.py
+++ b/solution.py
@@ -253,6 +253,9 @@
     placed, slots = transfers()
     order = SLOTS * width
     dma = pltpu.SemaphoreType.DMA
+    hcols, neighbours = (
+        pltpu.with_memory_space_constraint(each, pltpu.HBM) for each in (hcols, neighbours)
+    )
     return pl.pallas_call(
         functools.partial(kernel, n_cols, n_grp),
         out_shape=jax.ShapeDtypeStruct(hcols.shape, jnp.float32),
@@ -282,7 +285,7 @@
             dma((n_cols,)),
         ],
         compiler_params=pltpu.CompilerParams(
-            collective_id=0, has_side_effects=True, vmem_limit_bytes=63 * 1024 * 1024
+            collective_id=0, has_side_effects=True, vmem_limit_bytes=24 * 1024 * 1024
         ),
         name="density_columns",
     )(hcols, neighbours, counts)

time: 28.5 us -> 26.6 us (0.933)
  local copies, waits for them, and re-layouts: 1.92 us -> 0.82 us
  Pallas kernels: 25.5 us -> 24.7 us
    unnamed x1, local copies, waits for them, and re-layouts: 1.92 us -> 0.82 us
    pallas_call x1, Pallas kernels: 25.5 us -> 24.7 us  [shards(): pl.pallas_call(functools.partial(kernel, n_cols, n_grp), out_shape=jax.Sh...]
where the time goes in v3:
time: 26.6 us; the launch traced here: 26.2 us
  Pallas kernels  24.7 us (93%)
  local copies, waits for them, and re-layouts  0.82 us (3%)
  between operations  0.66 us (2%)
    pallas_call x1, Pallas kernels, shards(): pl.pallas_call(functools.partial(kernel, n_cols, n_grp), out_shape=jax.Sh...  24.7 us
    unnamed x1, local copies, waits for them, and re-layouts  0.82 us

profile of v3, /device:TPU:1, one launch (start us, length us, event | category | flops | bytes accessed | tf_op | source)
XLA Modules:
  0.0 26.2 jit_solution(4317638320346824728)
XLA Ops:
  0.7 24.7 %density_columns.1 = f32[1,1,9,128,128]{4,3,2,1,0:T(8,128)S(1)} custom-call(f32[1,1,9,128,128]{4,3,2,1,0:T(8,128)} %hcols.1, s32[1,1,6]{2,1,0:T(1,128)} %nbr_hbm.1, s32[1,1]{1,0:T(1,128)S(6)} %copy.5.cnt_hbm), custom_call_target="tpu_custom_call" | custom-call | tf_op jit(solution)/shard_map/density_columns/pallas_call | solution.py:259
  25.3 0.8 %copy.6 = f32[1,1,9,128,128]{4,3,2,1,0:T(8,128)} copy(f32[1,1,9,128,128]{4,3,2,1,0:T(8,128)S(1)} %density_columns.1) | data formatting | bytes 1179648

commit v4 on v3

--- a/solution.py
+++ b/solution.py
@@ -82,11 +82,6 @@
 
     lax.fori_loop(1, n_grp, greet_row, 0)
     lax.fori_loop(1, n_cols, greet_col, 0)
-    for step_cols in (-1, 1):
-        for step_grp in (-1, 1):
-            pl.semaphore_signal(
-                barrier, inc=1, device_id=at(step_cols, step_grp), device_id_type=MESH
-            )
     for i, value in enumerate(lookup(placed)):
         table[i] = jnp.int32(value)
     even = 1 - odd
@@ -103,7 +98,7 @@
         part = blk[k]
         own = own + jnp.sum((part * part).reshape(width // 8, 8, width), axis=0)
     row_sums[0] = own
-    pl.semaphore_wait(barrier, n_grp + n_cols + 2)
+    pl.semaphore_wait(barrier, n_grp + n_cols - 2)
 
     def row_copy(i):
         return pltpu.make_async_remote_copy(
@@ -152,8 +147,6 @@
 
     whole_edge = push(3, pick(straight[1], straight[-1]), 3, -side, 0)
     half_edge = push(3 + odd, pick(straight[-1], straight[1]) + odd, 2, side, 0)
-    for step_cols in (-1, 1):
-        push(4, pick(corner[-step_cols, 1], corner[-step_cols, -1]), 1, step_cols, -side)
     for offset, first, blocks, slot in placed:
         if offset[0] == 0:
             push(first, slot, blocks, 0, -offset[1])
@@ -178,7 +171,11 @@
     push(
         pick(straight[1] + 2, straight[-1]), pick(straight[1], straight[-1] + 2), 1, 0, side
     )
+    push(pick(straight[1] + 1, straight[-1] + 1), pick(corner[1, 1], corner[-1, -1]), 1, 0, -side)
     half_edge.wait_recv()
+    push(
+        pick(straight[-1] + 1, straight[1] + 1), pick(corner[-1, 1], corner[1, -1]), 1, 0, -side
+    )
     push(
         pick(straight[-1] + 1, straight[1] + 1), pick(corner[-1, -1], corner[1, 1]), 1, 0, side
     )

time: 26.6 us -> 26.2 us (0.985)
  no operation moved by 1% of the time
where the time goes in v4:
time: 26.2 us; the launch traced here: 26 us
  Pallas kernels  24.5 us (94%)
  local copies, waits for them, and re-layouts  0.82 us (3%)
  between operations  0.66 us (3%)
    pallas_call x1, Pallas kernels, shards(): pl.pallas_call(functools.partial(kernel, n_cols, n_grp), out_shape=jax.Sh...  24.5 us
    unnamed x1, local copies, waits for them, and re-layouts  0.82 us

profile of v4, /device:TPU:1, one launch (start us, length us, event | category | flops | bytes accessed | tf_op | source)
XLA Modules:
  0.0 26.0 jit_solution(15879248900358819782)
XLA Ops:
  0.7 24.5 %density_columns.1 = f32[1,1,9,128,128]{4,3,2,1,0:T(8,128)S(1)} custom-call(f32[1,1,9,128,128]{4,3,2,1,0:T(8,128)} %hcols.1, s32[1,1,6]{2,1,0:T(1,128)} %nbr_hbm.1, s32[1,1]{1,0:T(1,128)S(6)} %copy.5.cnt_hbm), custom_call_target="tpu_custom_call" | custom-call | tf_op jit(solution)/shard_map/density_columns/pallas_call | solution.py:256
  25.2 0.8 %copy.6 = f32[1,1,9,128,128]{4,3,2,1,0:T(8,128)} copy(f32[1,1,9,128,128]{4,3,2,1,0:T(8,128)S(1)} %density_columns.1) | data formatting | bytes 1179648

commit v5 on v4

--- a/solution.py
+++ b/solution.py
@@ -145,8 +145,11 @@
     def pick(at_even, at_odd):
         return at_even + (at_odd - at_even) * odd
 
-    whole_edge = push(3, pick(straight[1], straight[-1]), 3, -side, 0)
-    half_edge = push(3 + odd, pick(straight[-1], straight[1]) + odd, 2, side, 0)
+    centre = push(4, pick(straight[1] + 1, straight[-1] + 1), 1, -side, 0)
+    opposite = push(4, pick(straight[-1] + 1, straight[1] + 1), 1, side, 0)
+    shared = push(pick(5, 3), pick(straight[1] + 2, straight[-1]), 1, -side, 0)
+    push(pick(3, 5), pick(straight[1], straight[-1] + 2), 1, -side, 0)
+    push(pick(3, 5), pick(straight[-1], straight[1] + 2), 1, side, 0)
     for offset, first, blocks, slot in placed:
         if offset[0] == 0:
             push(first, slot, blocks, 0, -offset[1])
@@ -164,23 +167,19 @@
         high[rows, columns] = top
         low[rows, columns] = (value - top.astype(jnp.float32)).astype(jnp.bfloat16)
 
-    whole_edge.wait_recv()
-    push(
-        pick(straight[1] + 1, straight[-1] + 1), pick(corner[1, -1], corner[-1, 1]), 1, 0, side
-    )
-    push(
-        pick(straight[1] + 2, straight[-1]), pick(straight[1], straight[-1] + 2), 1, 0, side
-    )
-    push(pick(straight[1] + 1, straight[-1] + 1), pick(corner[1, 1], corner[-1, -1]), 1, 0, -side)
-    half_edge.wait_recv()
-    push(
-        pick(straight[-1] + 1, straight[1] + 1), pick(corner[-1, 1], corner[1, -1]), 1, 0, -side
-    )
-    push(
-        pick(straight[-1] + 1, straight[1] + 1), pick(corner[-1, -1], corner[1, 1]), 1, 0, side
-    )
+    centre.wait_recv()
+    held = pick(straight[1] + 1, straight[-1] + 1)
+    push(held, pick(corner[1, 1], corner[-1, -1]), 1, 0, -side)
+    push(held, pick(corner[1, -1], corner[-1, 1]), 1, 0, side)
+    opposite.wait_recv()
+    held = pick(straight[-1] + 1, straight[1] + 1)
+    push(held, pick(corner[-1, 1], corner[1, -1]), 1, 0, -side)
+    push(held, pick(corner[-1, -1], corner[1, 1]), 1, 0, side)
+    shared.wait_recv()
+    push(pick(straight[1] + 2, straight[-1]), pick(straight[1], straight[-1] + 2), 1, 0, side)
+    relayed = (centre, opposite, shared)
     for copy in copies:
-        if copy is not whole_edge and copy is not half_edge:
+        if all(copy is not done for done in relayed):
             copy.wait_recv()
 
     for p in range(SLOTS):
@@ -274,8 +273,8 @@
             pltpu.VMEM((n_cols, 8, width), jnp.float32),
             dma((2,)),
             dma,
-            dma((len(placed) + 1,)),
-            dma((len(placed) + 1,)),
+            dma((len(placed) + 4,)),
+            dma((len(placed) + 4,)),
             dma((n_grp,)),
             dma((n_grp,)),
             dma((n_cols,)),

time: 26.2 us -> 25.4 us (0.969)
  Pallas kernels: 24.5 us -> 23.7 us
    pallas_call x1, Pallas kernels: 24.5 us -> 23.7 us  [shards(): pl.pallas_call(functools.partial(kernel, n_cols, n_grp), out_shape=jax.Sh...]
where the time goes in v5:
time: 25.4 us; the launch traced here: 25.2 us
  Pallas kernels  23.7 us (93%)
  local copies, waits for them, and re-layouts  0.82 us (3%)
  between operations  0.66 us (3%)
    pallas_call x1, Pallas kernels, shards(): pl.pallas_call(functools.partial(kernel, n_cols, n_grp), out_shape=jax.Sh...  23.7 us
    unnamed x1, local copies, waits for them, and re-layouts  0.82 us

profile of v5, /device:TPU:1, one launch (start us, length us, event | category | flops | bytes accessed | tf_op | source)
XLA Modules:
  0.0 25.2 jit_solution(1840581418802236326)
XLA Ops:
  0.7 23.7 %density_columns.1 = f32[1,1,9,128,128]{4,3,2,1,0:T(8,128)S(1)} custom-call(f32[1,1,9,128,128]{4,3,2,1,0:T(8,128)} %hcols.1, s32[1,1,6]{2,1,0:T(1,128)} %nbr_hbm.1, s32[1,1]{1,0:T(1,128)S(6)} %copy.5.cnt_hbm), custom_call_target="tpu_custom_call" | custom-call | tf_op jit(solution)/shard_map/density_columns/pallas_call | solution.py:255
  24.4 0.8 %copy.6 = f32[1,1,9,128,128]{4,3,2,1,0:T(8,128)} copy(f32[1,1,9,128,128]{4,3,2,1,0:T(8,128)S(1)} %density_columns.1) | data formatting | bytes 1179648
